TPU v7x, 32 devices: a whole 2x2x4 slice. The times are simulated.
32 devices in a mesh: ctx: 8 (over z, core), heads: 4 (over y, x).
Axes of the slice: x: 2, y: 2, z: 4, core: 2. Of those that a mesh axis runs over, the one named last changes fastest.
Arguments:
- sharer_k: bfloat16 [8, 1024, 8192], P(None, 'ctx', 'heads'), may hold values from -6 to 6
- sharer_v: bfloat16 [8, 1024, 8192], P(None, 'ctx', 'heads'), may hold values from -6 to 6
- recv_k: bfloat16 [8, 1024, 8192], P('ctx', None, 'heads'), may hold values from -6 to 6
- recv_v: bfloat16 [8, 1024, 8192], P('ctx', None, 'heads'), may hold values from -6 to 6
- mixer_in: bfloat16 [4, 8192, 2, 512], P(None, 'heads'), may hold values from -0.03125 to 0.03125
- mixer_out: bfloat16 [2, 512, 8192], P(None, None, 'heads'), may hold values from -0.25 to 0.25
- mixer_gain: float32 [2, 64], P(None, 'heads'), may hold values from 0.5 to 2
- queries: bfloat16 [8, 256, 8192], P('ctx', None, 'heads'), may hold values from -40 to 40, as said below
- suffix_k: bfloat16 [8, 256, 8192], P('ctx', None, 'heads'), may hold values from -40 to 40, as said below
- suffix_v: bfloat16 [8, 256, 8192], P('ctx', None, 'heads'), may hold values from -6 to 6
- suffix_len: int32 [8], P('ctx'), may hold values from 64 to 256, as said below
- cache_offset: int32 [8], P('ctx'), may hold values from 512 to 1024, as said below
Outputs:
- attended: bfloat16 [8, 256, 8192], P('ctx', None, 'heads')
- merged_k: bfloat16 [8, 1024, 8192], P('ctx', None, 'heads')
- merged_v: bfloat16 [8, 1024, 8192], P('ctx', None, 'heads')
Inputs may be any that keep to these rules, and one draw needn't show every extreme that they name: Values of queries lie within this range. Values of suffix_k lie within this range. `suffix_len`: some request has 256 live rows and some has 64. Suffix row i of request r stands at position cache_offset[r] + i; some request sees all 1024 cached positions and some sees 1024 // 2.
All inputs are finite; a program needn't handle non-finite values.
Results may differ from a plain program's by a relative error of at most 0.0093.
Values may be sent and summed in bfloat16 or wider, within the bound.
A program may use at most 192 MiB of HBM per device.

v0:
```python
import functools
import math

import jax
import jax.numpy as jnp
from jax import lax
from jax.experimental import pallas as pl
from jax.experimental.pallas import tpu as pltpu
from jax.sharding import PartitionSpec as P

HD = 128


def merge_attend_kernel(
    offset_ref,
    length_ref,
    gain_ref,
    hidden_ref,
    out_w_ref,
    recv_k_ref,
    recv_v_ref,
    q_ref,
    suf_k_ref,
    suf_v_ref,
    att_ref,
    mk_ref,
    mv_ref,
    *,
    heads,
    row_block,
):
    request = pl.program_id(0)
    group = pl.program_id(1)
    ctx_total = mk_ref.shape[1]
    query_rows = q_ref.shape[1]
    offset = offset_ref[request]
    length = length_ref[request]
    scale = 1.0 / math.sqrt(HD)
    for member, (recv_ref, merged_ref) in enumerate(((recv_k_ref, mk_ref), (recv_v_ref, mv_ref))):
        for start in range(0, ctx_total, row_block):
            rows = pl.ds(start, row_block)
            delta = jnp.dot(
                hidden_ref[0, rows, :], out_w_ref[member], preferred_element_type=jnp.float32
            )
            for head in range(heads):
                cols = slice(head * HD, (head + 1) * HD)
                gain = gain_ref[member, group * heads + head]
                merged_ref[0, rows, cols] = (
                    recv_ref[0, rows, cols].astype(jnp.float32) + gain * delta[:, cols]
                ).astype(jnp.bfloat16)
    half = ctx_total // 2
    late_pos = half + lax.broadcasted_iota(jnp.int32, (1, ctx_total - half), 1)
    late_seen = late_pos < offset
    own_seen = lax.broadcasted_iota(jnp.int32, (query_rows, query_rows), 1) <= (
        lax.broadcasted_iota(jnp.int32, (query_rows, query_rows), 0)
    )
    alive = lax.broadcasted_iota(jnp.int32, (query_rows, 1), 0) < length
    contract = (((1,), (1,)), ((), ()))
    for head in range(heads):
        cols = slice(head * HD, (head + 1) * HD)
        query = q_ref[0, :, cols]

        def scores_of(keys):
            return lax.dot_general(query, keys, contract, preferred_element_type=jnp.float32)

        early = scores_of(mk_ref[0, :half, cols])
        late = jnp.where(late_seen, scores_of(mk_ref[0, half:, cols]), -jnp.inf)
        own = jnp.where(own_seen, scores_of(suf_k_ref[0, :, cols]), -jnp.inf)
        peak = jnp.maximum(
            jnp.maximum(
                jnp.max(early, axis=1, keepdims=True), jnp.max(late, axis=1, keepdims=True)
            ),
            jnp.max(own, axis=1, keepdims=True),
        )
        denom = None
        blended = None
        for part, values in (
            (early, mv_ref[0, :half, cols]),
            (late, mv_ref[0, half:, cols]),
            (own, suf_v_ref[0, :, cols]),
        ):
            numer = jnp.exp((part - peak) * scale)
            total = jnp.sum(numer, axis=1, keepdims=True)
            mixed = jnp.dot(
                numer.astype(jnp.bfloat16), values, preferred_element_type=jnp.float32
            )
            denom = total if denom is None else denom + total
            blended = mixed if blended is None else blended + mixed
        att_ref[0, :, cols] = jnp.where(alive, blended / denom, 0.0).astype(jnp.bfloat16)


def merge_attend(
    hidden, mixer_out, mixer_gain, recv_k, recv_v, queries, suffix_k, suffix_v, suffix_len, cache_offset
):
    requests, ctx_total, width = recv_k.shape
    query_rows = queries.shape[1]
    rank = hidden.shape[-1]
    heads = 2
    lanes = heads * HD
    row_block = min(256, ctx_total)

    def by_head(rows):
        return pl.BlockSpec((1, rows, lanes), lambda r, g: (r, 0, g))

    smem = pl.BlockSpec(memory_space=pltpu.SMEM)
    return pl.pallas_call(
        functools.partial(merge_attend_kernel, heads=heads, row_block=row_block),
        grid=(requests, width // lanes),
        in_specs=[
            smem,
            smem,
            smem,
            pl.BlockSpec((1, ctx_total, rank), lambda r, g: (r, 0, 0)),
            pl.BlockSpec((2, rank, lanes), lambda r, g: (0, 0, g)),
            by_head(ctx_total),
            by_head(ctx_total),
            by_head(query_rows),
            by_head(query_rows),
            by_head(query_rows),
        ],
        out_specs=[by_head(query_rows), by_head(ctx_total), by_head(ctx_total)],
        out_shape=[
            jax.ShapeDtypeStruct(queries.shape, jnp.bfloat16),
            jax.ShapeDtypeStruct(recv_k.shape, jnp.bfloat16),
            jax.ShapeDtypeStruct(recv_v.shape, jnp.bfloat16),
        ],
        compiler_params=pltpu.CompilerParams(
            dimension_semantics=("arbitrary", "arbitrary"), vmem_limit_bytes=48 * 1024 * 1024
        ),
        name="merge_attend",
    )(
        cache_offset,
        suffix_len,
        mixer_gain,
        hidden,
        mixer_out,
        recv_k,
        recv_v,
        queries,
        suffix_k,
        suffix_v,
    )


def exchange_kernel(
    sharer_k_ref,
    sharer_v_ref,
    recv_k_ref,
    recv_v_ref,
    w_hbm,
    out_ref,
    x_ref,
    packed_ref,
    w_ref,
    part_ref,
    landed_ref,
    passed_ref,
    share_ref,
    moved_ref,
    hidden_ref,
    x_sem,
    w_sem,
    sum_send,
    sum_recv,
    move_send,
    move_recv,
    gather_send,
    gather_recv,
    out_sem,
    *,
    ctx_size,
    head_size,
    chunks,
):
    my_ctx = lax.axis_index("ctx")
    my_head = lax.axis_index("heads")
    group = ctx_size // chunks
    block_rows, width = x_ref.shape[2:]
    rank = w_ref.shape[-1]
    sub = block_rows // head_size
    w_rows = math.gcd(width, 128)
    square = head_size == 4

    def ctx_of(shift):
        return lax.rem(my_ctx + shift + ctx_size, ctx_size)

    def head_of(shift):
        return lax.rem(my_head + shift, head_size)

    def x_copy(member, step):
        sharer = (sharer_k_ref, sharer_v_ref)[member]
        return pltpu.make_async_copy(
            sharer.at[ctx_of(1 + step)], x_ref.at[member, step], x_sem.at[member, step]
        )

    def y_copy(member, step):
        recv = (recv_k_ref, recv_v_ref)[member]
        return pltpu.make_async_copy(
            recv.at[ctx_of(-1 - step)],
            x_ref.at[member, ctx_size + step],
            x_sem.at[member, ctx_size + step],
        )

    def w_copy(slab):
        return pltpu.make_async_copy(w_hbm.at[slab], packed_ref.at[slab], w_sem.at[slab])

    def sum_copy(chunk, shift):
        target = head_of(shift)
        rows = pl.ds(chunk * group, group)
        return pltpu.make_async_remote_copy(
            src_ref=part_ref.at[rows, target],
            dst_ref=landed_ref.at[shift - 1, rows],
            send_sem=sum_send.at[chunk, shift - 1],
            recv_sem=sum_recv.at[chunk, shift - 1],
            device_id=(my_ctx, target),
            device_id_type=pl.DeviceIdType.MESH,
        )

    def pair_copy(chunk, stage, half):
        near = (my_head + 1 - 2 * lax.rem(my_head, 2), lax.rem(my_head + 2, 4))
        target, other = near[half], near[1 - half]
        rows = pl.ds(chunk * group, group)
        cols = pl.ds(half * rank, rank)
        if stage == 0:
            source = part_ref.at[rows, 3 - my_head, :, cols]
        elif stage == 1:
            source = part_ref.at[rows, target, :, cols]
        else:
            source, target = passed_ref.at[rows, :, cols], other
        return pltpu.make_async_remote_copy(
            src_ref=source,
            dst_ref=landed_ref.at[stage, rows, :, cols],
            send_sem=sum_send.at[chunk, 2 * stage + half],
            recv_sem=sum_recv.at[chunk, 2 * stage + half],
            device_id=(my_ctx, target),
            device_id_type=pl.DeviceIdType.MESH,
        )

    def pass_on(chunk):
        rows = pl.ds(chunk * group, group)
        near = (my_head + 1 - 2 * lax.rem(my_head, 2), lax.rem(my_head + 2, 4))
        for half in range(2):
            cols = slice(half * rank, (half + 1) * rank)
            pair_copy(chunk, 0, half).wait_recv()
            passed_ref[rows, :, cols] = (
                part_ref[rows, near[1 - half], :, cols].astype(jnp.float32)
                + landed_ref[0, rows, :, cols].astype(jnp.float32)
            ).astype(jnp.bfloat16)
            pair_copy(chunk, 2, half).start()

    def move_copy(step):
        return pltpu.make_async_remote_copy(
            src_ref=share_ref.at[step],
            dst_ref=moved_ref.at[step],
            send_sem=move_send.at[step],
            recv_sem=move_recv.at[step],
            device_id=(ctx_of(1 + step), my_head),
            device_id_type=pl.DeviceIdType.MESH,
        )

    def gather_copy(chunk, shift):
        block = hidden_ref.at[pl.ds(chunk * group, group), my_head]
        return pltpu.make_async_remote_copy(
            src_ref=block,
            dst_ref=block,
            send_sem=gather_send.at[chunk, shift - 1],
            recv_sem=gather_recv.at[chunk, shift - 1],
            device_id=(my_ctx, head_of(shift)),
            device_id_type=pl.DeviceIdType.MESH,
        )

    def summed(chunk):
        rows = pl.ds(chunk * group, group)
        if square:
            total = part_ref[rows, my_head].astype(jnp.float32)
            for stage in (1, 2):
                for half in range(2):
                    pair_copy(chunk, stage, half).wait_recv()
                total = total + landed_ref[stage, rows].astype(jnp.float32)
            return total
        for shift in range(1, head_size):
            sum_copy(chunk, shift).wait_recv()
        total = part_ref[rows, my_head].astype(jnp.float32)
        for shift in range(1, head_size):
            total = total + landed_ref[shift - 1, rows].astype(jnp.float32)
        return total

    w_copy(0).start()
    for step in range(ctx_size):
        for member in range(2):
            x_copy(member, step).start()
        if step == group - 1:
            w_copy(1).start()
    for slab in range(2, 4):
        w_copy(slab).start()
    for step in range(ctx_size):
        for member in range(2):
            y_copy(member, step).start()

    barrier = pltpu.get_barrier_semaphore()
    for shift in range(1, head_size):
        pl.semaphore_signal(
            barrier,
            inc=1,
            device_id=(my_ctx, head_of(shift)),
            device_id_type=pl.DeviceIdType.MESH,
        )
    for shift in range(1, ctx_size):
        pl.semaphore_signal(
            barrier,
            inc=1,
            device_id=(ctx_of(shift), my_head),
            device_id_type=pl.DeviceIdType.MESH,
        )
    pl.semaphore_wait(barrier, head_size - 1 + ctx_size - 1)

    def project(chunk, _):
        side = chunk // chunks

        @pl.when(lax.rem(chunk, chunks) == 0)
        def _():
            for member in range(2):
                slab = 2 * side + member
                pltpu.make_async_copy(w_hbm.at[0], packed_ref.at[slab], w_sem.at[slab]).wait()

                def split(part, _):
                    band = pl.ds(part * w_rows, w_rows)
                    for col in range(rank // 128):
                        cols = slice(col * 128, (col + 1) * 128)
                        pair = packed_ref[slab, band, :, cols].astype(jnp.float32)
                        for half in range(2):
                            w_ref[member, half, band, cols] = pair[:, half].astype(jnp.bfloat16)
                    return 0

                lax.fori_loop(0, width // w_rows, split, 0)

        for extra in range(group):
            for member in range(2):
                step = chunk * group + extra
                pltpu.make_async_copy(
                    recv_k_ref.at[0], x_ref.at[member, step], x_sem.at[member, step]
                ).wait()
        rows = pl.ds(chunk * group, group)
        for half in range(2):
            total = None
            for member in range(2):
                term = jnp.dot(
                    x_ref[member, rows].reshape(group * block_rows, width),
                    w_ref[member, half],
                    preferred_element_type=jnp.float32,
                )
                total = term if total is None else total + term
            part_ref[rows, :, :, half * rank : (half + 1) * rank] = total.astype(
                jnp.bfloat16
            ).reshape(group, head_size, sub, rank)
        if square:
            for stage in range(2):
                for half in range(2):
                    pair_copy(chunk, stage, half).start()

            @pl.when(chunk >= 1)
            def _():
                pass_on(chunk - 1)
        else:
            for shift in range(1, head_size):
                sum_copy(chunk, shift).start()

        @pl.when(chunk >= chunks)
        def _():
            first = chunk - chunks
            total = summed(first).astype(jnp.bfloat16)
            share_ref[pl.ds(first * group, group)] = total

            for extra in range(group):
                step = first * group + extra

                @pl.when(step < ctx_size - 1)
                def _():
                    move_copy(step).start()

        return 0

    lax.fori_loop(0, 2 * chunks, project, 0)
    if square:
        pass_on(2 * chunks - 1)

    def finish(chunk, _):
        total = summed(chunk + chunks)
        for extra in range(group):
            step = chunk * group + extra

            @pl.when(step < ctx_size - 1)
            def _():
                move_copy(step).wait_recv()

            @pl.when(step == ctx_size - 1)
            def _():
                moved_ref[ctx_size - 1] = share_ref[ctx_size - 1]

        rows = pl.ds(chunk * group, group)
        total = total + moved_ref[rows].astype(jnp.float32)
        gate, up = total[..., :rank], total[..., rank:]
        hidden_ref[rows, my_head] = (gate / (1.0 + jnp.exp(-gate)) * up).astype(jnp.bfloat16)
        for shift in range(1, head_size):
            gather_copy(chunk, shift).start()
        return 0

    lax.fori_loop(0, chunks, finish, 0)

    def out_copy(step):
        return pltpu.make_async_copy(
            hidden_ref.at[step], out_ref.at[ctx_of(-1 - step)], out_sem.at[step]
        )

    def deliver(chunk, _):
        for shift in range(1, head_size):
            source = head_of(head_size - shift)
            block = hidden_ref.at[pl.ds(chunk * group, group), source]
            pltpu.make_async_remote_copy(
                src_ref=block,
                dst_ref=block,
                send_sem=gather_send.at[chunk, shift - 1],
                recv_sem=gather_recv.at[chunk, shift - 1],
                device_id=(my_ctx, head_of(shift)),
                device_id_type=pl.DeviceIdType.MESH,
            ).wait_recv()
        for extra in range(group):
            out_copy(chunk * group + extra).start()
        return 0

    lax.fori_loop(0, chunks, deliver, 0)

    def drain(chunk, _):
        if square:
            for stage in range(3):
                for half in range(2):
                    pair_copy(chunk, stage, half).wait_send()
                    pair_copy(chunk + chunks, stage, half).wait_send()
        for shift in range(1, head_size):
            if not square:
                sum_copy(chunk, shift).wait_send()
                sum_copy(chunk + chunks, shift).wait_send()
            gather_copy(chunk, shift).wait_send()
        for extra in range(group):
            step = chunk * group + extra

            @pl.when(step < ctx_size - 1)
            def _():
                move_copy(step).wait_send()

            out_copy(step).wait()
        return 0

    lax.fori_loop(0, chunks, drain, 0)


def exchange(sharer_k, sharer_v, recv_k, recv_v, weights, ctx_size, head_size):
    _, block_rows, width = sharer_k.shape
    rank = weights.shape[-1]
    sub = block_rows // head_size
    chunks = math.gcd(ctx_size, 4)
    blocks = (ctx_size, block_rows, width)
    anywhere = pl.BlockSpec(memory_space=pl.ANY)
    dma = pltpu.SemaphoreType.DMA
    bf16 = jnp.bfloat16
    return pl.pallas_call(
        functools.partial(
            exchange_kernel, ctx_size=ctx_size, head_size=head_size, chunks=chunks
        ),
        in_specs=[anywhere] * 5,
        out_specs=anywhere,
        out_shape=jax.ShapeDtypeStruct((ctx_size, head_size, sub, rank), bf16),
        scratch_shapes=[
            pltpu.VMEM((2, 2 * ctx_size, block_rows, width), bf16),
            pltpu.VMEM((4, width, 2, rank), bf16),
            pltpu.VMEM((2, 2, width, rank), bf16),
            pltpu.VMEM((2 * ctx_size, head_size, sub, 2 * rank), bf16),
            pltpu.VMEM((head_size - 1, 2 * ctx_size, sub, 2 * rank), bf16),
            pltpu.VMEM((2 * ctx_size, sub, 2 * rank), bf16),
            pltpu.VMEM((ctx_size, sub, 2 * rank), bf16),
            pltpu.VMEM((ctx_size, sub, 2 * rank), bf16),
            pltpu.VMEM((ctx_size, head_size, sub, rank), bf16),
            dma((2, 2 * ctx_size)),
            dma((4,)),
            dma((2 * chunks, max(6, head_size - 1))),
            dma((2 * chunks, max(6, head_size - 1))),
            dma((ctx_size,)),
            dma((ctx_size,)),
            dma((chunks, head_size - 1)),
            dma((chunks, head_size - 1)),
            dma((ctx_size,)),
        ],
        compiler_params=pltpu.CompilerParams(
            collective_id=0, has_side_effects=True, vmem_limit_bytes=60 * 1024 * 1024
        ),
        name="exchange",
    )(sharer_k, sharer_v, recv_k.reshape(blocks), recv_v.reshape(blocks), weights)


def local(
    sharer_k,
    sharer_v,
    recv_k,
    recv_v,
    mixer_in,
    mixer_out,
    mixer_gain,
    queries,
    suffix_k,
    suffix_v,
    suffix_len,
    cache_offset,
):
    requests, ctx_total, width = recv_k.shape
    rank = mixer_in.shape[3]
    hidden = exchange(
        sharer_k,
        sharer_v,
        recv_k,
        recv_v,
        mixer_in,
        lax.axis_size("ctx"),
        lax.axis_size("heads"),
    )
    hidden = hidden.reshape(requests, ctx_total, rank)
    return tuple(
        merge_attend(
            hidden,
            mixer_out,
            mixer_gain,
            recv_k,
            recv_v,
            queries,
            suffix_k,
            suffix_v,
            suffix_len,
            cache_offset,
        )
    )


def solution(mesh):
    cache = P("ctx", None, "heads")
    placed = (
        P(None, "ctx", "heads"),
        P(None, "ctx", "heads"),
        cache,
        cache,
        P(None, "heads", None, None),
        P(None, None, "heads"),
        P(None, "heads"),
        cache,
        cache,
        cache,
        P("ctx"),
        P("ctx"),
    )
    return jax.shard_map(
        local, mesh=mesh, in_specs=placed, out_specs=(cache, cache, cache), check_vma=False
    )
```

profile of v0, /device:TPU:0, one launch (start us, length us, event | category | flops | bytes accessed | tf_op | source)
XLA Modules:
  0.0 101.4 jit_solution(13149112422907918617)
XLA Ops:
  1.9 0.0 copy-start.1
  1.9 0.0 copy-start.2
  1.9 0.0 copy-start.3
  2.0 0.0 copy-start.4
  2.0 79.9 %exchange.1 = bf16[8,4,32,512]{3,2,1,0:T(8,128)(2,1)} custom-call(bf16[8,128,2048]{2,1,0:T(8,128)(2,1)} %sharer_k_ref.1, bf16[8,128,2048]{2,1,0:T(8,128)(2,1)} %sharer_v_ref.1, bf16[8,128,2048]{2,1,0:T(8,128)(2,1)} %bitcast.4, bf16[8,128,2048]{2,1,0:T(8,128)(2,1)} %bitcast.5, bf16[4,2048,2,512]{3,2,1,0:T(2,128)(2,1)} %w_hbm.1), custom_call_target="tpu_custom_call" | custom-call | tf_op jit(solution)/shard_map/exchange/pallas_call | solution.py:466
  81.9 0.0 copy-done.1
  81.9 0.0 copy-done.2
  81.9 0.0 copy-done.3
  81.9 0.0 copy-done.4
  82.0 0.0 copy-start
  82.0 1.2 %copy-done = bf16[8,4,32,512]{3,2,1,0:T(8,128)(2,1)S(1)} copy-done((bf16[8,4,32,512]{3,2,1,0:T(8,128)(2,1)S(1)}, bf16[8,4,32,512]{3,2,1,0:T(8,128)(2,1)}, u32[]{:S(2)}) %copy-start) | copy-done | bytes 1048600
  83.2 18.2 %merge_attend.1 = (bf16[1,256,2048]{2,1,0:T(8,128)(2,1)}, bf16[1,1024,2048]{2,1,0:T(8,128)(2,1)}, bf16[1,1024,2048]{2,1,0:T(8,128)(2,1)}) custom-call(s32[1]{0:T(128)S(6)} %copy.16.offset_ref, s32[1]{0:T(128)S(6)} %copy.15.length_ref, f32[2,16]{1,0:T(2,128)S(1)} %copy-done.4, bf16[1,1024,512]{2,1,0:T(8,128)(2,1)S(1)} %bitcast.3, ...), custom_call_target="tpu_custom_call" | custom-call | tf_op jit(solution)/shard_map/merge_attend/pallas_call | solution.py:106
Async XLA Ops:
  1.9 80.0 %copy-start.1 = (bf16[1,256,2048]{2,1,0:T(8,128)(2,1)S(1)}, bf16[1,256,2048]{2,1,0:T(8,128)(2,1)}, u32[]{:S(2)}) copy-start(bf16[1,256,2048]{2,1,0:T(8,128)(2,1)} %q_ref.1) | copy-start | bytes 3145732
  1.9 80.0 %copy-start.2 = (bf16[1,256,2048]{2,1,0:T(8,128)(2,1)S(1)}, bf16[1,256,2048]{2,1,0:T(8,128)(2,1)}, u32[]{:S(2)}) copy-start(bf16[1,256,2048]{2,1,0:T(8,128)(2,1)} %suf_k_ref.1) | copy-start | bytes 3145732
  1.9 80.0 %copy-start.3 = (bf16[1,256,2048]{2,1,0:T(8,128)(2,1)S(1)}, bf16[1,256,2048]{2,1,0:T(8,128)(2,1)}, u32[]{:S(2)}) copy-start(bf16[1,256,2048]{2,1,0:T(8,128)(2,1)} %suf_v_ref.1) | copy-start | bytes 3145732
  2.0 80.0 %copy-start.4 = (f32[2,16]{1,0:T(2,128)S(1)}, f32[2,16]{1,0:T(2,128)}, u32[]{:S(2)}) copy-start(f32[2,16]{1,0:T(2,128)} %gain_ref.1) | copy-start | bytes 388
  82.0 1.2 %copy-start = (bf16[8,4,32,512]{3,2,1,0:T(8,128)(2,1)S(1)}, bf16[8,4,32,512]{3,2,1,0:T(8,128)(2,1)}, u32[]{:S(2)}) copy-start(bf16[8,4,32,512]{3,2,1,0:T(8,128)(2,1)} %exchange.1) | copy-start | bytes 3145732
where the time goes:
time: 102 us; the launch traced here: 101 us
  Pallas kernels  98.2 us (96%)
  between operations  2.01 us (2%)
  local copies, waits for them, and re-layouts  1.23 us (1%)
    pallas_call x1, Pallas kernels, exchange(): pl.pallas_call(functools.partial(exchange_kernel, ctx_size=ctx_size, head...  79.9 us
    pallas_call x1, Pallas kernels, merge_attend(): pl.pallas_call(functools.partial(merge_attend_kernel, heads=heads, row_bl...  18.2 us

commit v1 on v0

--- a/solution.py
+++ b/solution.py
@@ -180,6 +180,7 @@
     sub = block_rows // head_size
     w_rows = math.gcd(width, 128)
     square = head_size == 4
+    flat_ref = packed_ref.reshape(4, 2 * width, rank)
 
     def ctx_of(shift):
         return lax.rem(my_ctx + shift + ctx_size, ctx_size)
@@ -324,12 +325,11 @@
                 pltpu.make_async_copy(w_hbm.at[0], packed_ref.at[slab], w_sem.at[slab]).wait()
 
                 def split(part, _):
+                    pairs = flat_ref[slab, pl.ds(part * 2 * w_rows, 2 * w_rows), :]
+                    halves = pltpu.einshape("(kh)l->hkl", pairs, h=2)
                     band = pl.ds(part * w_rows, w_rows)
-                    for col in range(rank // 128):
-                        cols = slice(col * 128, (col + 1) * 128)
-                        pair = packed_ref[slab, band, :, cols].astype(jnp.float32)
-                        for half in range(2):
-                            w_ref[member, half, band, cols] = pair[:, half].astype(jnp.bfloat16)
+                    for half in range(2):
+                        w_ref[member, half, band, :] = halves[half]
                     return 0
 
                 lax.fori_loop(0, width // w_rows, split, 0)
@@ -497,6 +497,426 @@
     )(sharer_k, sharer_v, recv_k.reshape(blocks), recv_v.reshape(blocks), weights)
 
 
+def near_exchange_kernel(
+    sharer_k_ref,
+    sharer_v_ref,
+    recv_k_ref,
+    recv_v_ref,
+    w_hbm,
+    out_ref,
+    x_ref,
+    packed_ref,
+    w_ref,
+    part_ref,
+    landed_ref,
+    passed_ref,
+    share_ref,
+    moved_ref,
+    hidden_ref,
+    raw_ref,
+    x_sem,
+    w_sem,
+    sum_send,
+    sum_recv,
+    raw_send,
+    raw_recv,
+    move_send,
+    move_recv,
+    gather_send,
+    gather_recv,
+    out_sem,
+    *,
+    ctx_size,
+    head_size,
+):
+    my_ctx = lax.axis_index("ctx")
+    my_head = lax.axis_index("heads")
+    group = 2
+    chunks = ctx_size // group
+    far = ctx_size - 4
+    far_chunks = far // group
+    hoods = ctx_size // 4
+    hood = my_ctx // 4
+    seat = lax.rem(my_ctx, 4)
+    near = (my_head + 1 - 2 * lax.rem(my_head, 2), lax.rem(my_head + 2, 4))
+    block_rows, width = x_ref.shape[2:]
+    rank = w_ref.shape[-1]
+    sub = block_rows // head_size
+    w_rows = math.gcd(width, 128)
+    flat_ref = packed_ref.reshape(4, 2 * width, rank)
+
+    def ctx_of(shift):
+        return lax.rem(my_ctx + shift, ctx_size)
+
+    def target_of(step):
+        other = lax.rem(hood + 1 + step // 4, hoods)
+        return other * 4 + lax.rem(seat + lax.rem(step + 2, 4), 4)
+
+    def source_of(step):
+        other = lax.rem(hood + 2 * hoods - 1 - step // 4, hoods)
+        return other * 4 + lax.rem(seat + 4 - lax.rem(step + 2, 4), 4)
+
+    def head_of(shift):
+        return lax.rem(my_head + shift, head_size)
+
+    def x_copy(member, step):
+        sharer = (sharer_k_ref, sharer_v_ref)[member]
+        return pltpu.make_async_copy(
+            sharer.at[target_of(step)], x_ref.at[member, step], x_sem.at[member, step]
+        )
+
+    def y_copy(member, step):
+        recv = (recv_k_ref, recv_v_ref)[member]
+        return pltpu.make_async_copy(
+            recv.at[source_of(step)],
+            x_ref.at[member, ctx_size + step],
+            x_sem.at[member, ctx_size + step],
+        )
+
+    def w_copy(slab):
+        return pltpu.make_async_copy(w_hbm.at[slab], packed_ref.at[slab], w_sem.at[slab])
+
+    def pair_copy(chunk, stage, half):
+        target, other = near[half], near[1 - half]
+        rows = pl.ds(chunk * group, group)
+        cols = pl.ds(half * rank, rank)
+        if stage == 0:
+            source = part_ref.at[rows, 3 - my_head, :, cols]
+        elif stage == 1:
+            source = part_ref.at[rows, target, :, cols]
+        else:
+            source, target = passed_ref.at[rows, :, cols], other
+        return pltpu.make_async_remote_copy(
+            src_ref=source,
+            dst_ref=landed_ref.at[stage, rows, :, cols],
+            send_sem=sum_send.at[chunk, 2 * stage + half],
+            recv_sem=sum_recv.at[chunk, 2 * stage + half],
+            device_id=(my_ctx, target),
+            device_id_type=pl.DeviceIdType.MESH,
+        )
+
+    def pass_on(chunk):
+        rows = pl.ds(chunk * group, group)
+        for half in range(2):
+            cols = slice(half * rank, (half + 1) * rank)
+            pair_copy(chunk, 0, half).wait_recv()
+            passed_ref[rows, :, cols] = (
+                part_ref[rows, near[1 - half], :, cols].astype(jnp.float32)
+                + landed_ref[0, rows, :, cols].astype(jnp.float32)
+            ).astype(jnp.bfloat16)
+            pair_copy(chunk, 2, half).start()
+
+    def move_copy(step):
+        return pltpu.make_async_remote_copy(
+            src_ref=share_ref.at[step],
+            dst_ref=moved_ref.at[step],
+            send_sem=move_send.at[step],
+            recv_sem=move_recv.at[step],
+            device_id=(target_of(step), my_head),
+            device_id_type=pl.DeviceIdType.MESH,
+        )
+
+    def raw_copy(step):
+        return pltpu.make_async_remote_copy(
+            src_ref=part_ref.at[step],
+            dst_ref=raw_ref.at[step - far],
+            send_sem=raw_send.at[step - far],
+            recv_sem=raw_recv.at[step - far],
+            device_id=(target_of(step), my_head),
+            device_id_type=pl.DeviceIdType.MESH,
+        )
+
+    def gather_copy(chunk, side):
+        block = hidden_ref.at[pl.ds(chunk * group, group), my_head]
+        return pltpu.make_async_remote_copy(
+            src_ref=block,
+            dst_ref=block,
+            send_sem=gather_send.at[chunk, side],
+            recv_sem=gather_recv.at[chunk, side],
+            device_id=(my_ctx, near[side]),
+            device_id_type=pl.DeviceIdType.MESH,
+        )
+
+    def arrived_copy(chunk, side):
+        block = hidden_ref.at[pl.ds(chunk * group, group), near[side]]
+        return pltpu.make_async_remote_copy(
+            src_ref=block,
+            dst_ref=block,
+            send_sem=gather_send.at[chunk, side],
+            recv_sem=gather_recv.at[chunk, side],
+            device_id=(my_ctx, near[side]),
+            device_id_type=pl.DeviceIdType.MESH,
+        )
+
+    def relay_copy(chunk, half, owner):
+        cols = pl.ds(half * (rank // 2), rank // 2)
+        block = hidden_ref.at[pl.ds(chunk * group, group), owner, :, cols]
+        return pltpu.make_async_remote_copy(
+            src_ref=block,
+            dst_ref=block,
+            send_sem=gather_send.at[chunk, 2 + half],
+            recv_sem=gather_recv.at[chunk, 2 + half],
+            device_id=(my_ctx, near[1 - half]),
+            device_id_type=pl.DeviceIdType.MESH,
+        )
+
+    def relay(chunk):
+        for half in range(2):
+            arrived_copy(chunk, half).wait_recv()
+            relay_copy(chunk, half, near[half]).start()
+
+    def summed(chunk):
+        rows = pl.ds(chunk * group, group)
+        total = part_ref[rows, my_head].astype(jnp.float32)
+        for stage in (1, 2):
+            for half in range(2):
+                pair_copy(chunk, stage, half).wait_recv()
+            total = total + landed_ref[stage, rows].astype(jnp.float32)
+        return total
+
+    w_copy(0).start()
+    for step in range(ctx_size):
+        for member in range(2):
+            x_copy(member, step).start()
+        if step == group - 1:
+            w_copy(1).start()
+    for slab in range(2, 4):
+        w_copy(slab).start()
+    for step in range(ctx_size):
+        for member in range(2):
+            y_copy(member, step).start()
+
+    barrier = pltpu.get_barrier_semaphore()
+    for shift in range(1, head_size):
+        pl.semaphore_signal(
+            barrier,
+            inc=1,
+            device_id=(my_ctx, head_of(shift)),
+            device_id_type=pl.DeviceIdType.MESH,
+        )
+    for shift in range(1, ctx_size):
+        pl.semaphore_signal(
+            barrier,
+            inc=1,
+            device_id=(ctx_of(shift), my_head),
+            device_id_type=pl.DeviceIdType.MESH,
+        )
+    pl.semaphore_wait(barrier, head_size - 1 + ctx_size - 1)
+
+    def project(chunk, _):
+        side = chunk // chunks
+
+        @pl.when(lax.rem(chunk, chunks) == 0)
+        def _():
+            for member in range(2):
+                slab = 2 * side + member
+                pltpu.make_async_copy(w_hbm.at[0], packed_ref.at[slab], w_sem.at[slab]).wait()
+
+                def split(part, _):
+                    pairs = flat_ref[slab, pl.ds(part * 2 * w_rows, 2 * w_rows), :]
+                    halves = pltpu.einshape("(kh)l->hkl", pairs, h=2)
+                    band = pl.ds(part * w_rows, w_rows)
+                    for half in range(2):
+                        w_ref[member, half, band, :] = halves[half]
+                    return 0
+
+                lax.fori_loop(0, width // w_rows, split, 0)
+
+        for extra in range(group):
+            for member in range(2):
+                step = chunk * group + extra
+                pltpu.make_async_copy(
+                    recv_k_ref.at[0], x_ref.at[member, step], x_sem.at[member, step]
+                ).wait()
+        rows = pl.ds(chunk * group, group)
+        for half in range(2):
+            total = None
+            for member in range(2):
+                term = jnp.dot(
+                    x_ref[member, rows].reshape(group * block_rows, width),
+                    w_ref[member, half],
+                    preferred_element_type=jnp.float32,
+                )
+                total = term if total is None else total + term
+            part_ref[rows, :, :, half * rank : (half + 1) * rank] = total.astype(
+                jnp.bfloat16
+            ).reshape(group, head_size, sub, rank)
+        @pl.when(chunk >= 2 * chunks - 2)
+        def _():
+            for extra in range(group):
+                step = (chunk - chunks) * group + extra
+                slot = ctx_size + step
+
+                def add(other):
+                    part_ref[slot] = (
+                        part_ref[slot].astype(jnp.float32) + other.astype(jnp.float32)
+                    ).astype(jnp.bfloat16)
+
+                @pl.when(step == ctx_size - 2)
+                def _():
+                    add(part_ref[ctx_size - 2])
+
+                @pl.when(step != ctx_size - 2)
+                def _():
+                    raw_copy(step).wait_recv()
+                    add(raw_ref[step - far])
+
+        is_near = jnp.logical_and(chunk >= far_chunks, chunk < chunks)
+
+        @pl.when(jnp.logical_not(is_near))
+        def _():
+            for stage in range(2):
+                for half in range(2):
+                    pair_copy(chunk, stage, half).start()
+
+        @pl.when(is_near)
+        def _():
+            for extra in range(group):
+                step = chunk * group + extra
+
+                @pl.when(step != ctx_size - 2)
+                def _():
+                    raw_copy(step).start()
+
+        last = chunk - 1
+
+        @pl.when(
+            jnp.logical_or(jnp.logical_and(last >= 0, last < far_chunks), last >= chunks)
+        )
+        def _():
+            pass_on(last)
+
+        @pl.when(jnp.logical_and(chunk >= chunks, chunk < chunks + far_chunks))
+        def _():
+            first = chunk - chunks
+            total = summed(first).astype(jnp.bfloat16)
+            share_ref[pl.ds(first * group, group)] = total
+            for extra in range(group):
+                move_copy(first * group + extra).start()
+
+        return 0
+
+    lax.fori_loop(0, 2 * chunks, project, 0)
+    pass_on(2 * chunks - 1)
+
+    def activate(chunk, total):
+        gate, up = total[..., :rank], total[..., rank:]
+        hidden_ref[pl.ds(chunk * group, group), my_head] = (
+            gate / (1.0 + jnp.exp(-gate)) * up
+        ).astype(jnp.bfloat16)
+        for side in range(2):
+            gather_copy(chunk, side).start()
+
+    def finish(chunk, _):
+        total = summed(chunk + chunks)
+
+        @pl.when(chunk < far_chunks)
+        def _():
+            for extra in range(group):
+                move_copy(chunk * group + extra).wait_recv()
+            moved = moved_ref[pl.ds(chunk * group, group)].astype(jnp.float32)
+            activate(chunk, total + moved)
+
+        @pl.when(chunk >= far_chunks)
+        def _():
+            activate(chunk, total)
+
+        @pl.when(chunk >= 1)
+        def _():
+            relay(chunk - 1)
+
+        return 0
+
+    lax.fori_loop(0, chunks, finish, 0)
+    relay(chunks - 1)
+
+    def out_copy(step):
+        return pltpu.make_async_copy(
+            hidden_ref.at[step], out_ref.at[source_of(step)], out_sem.at[step]
+        )
+
+    def deliver(chunk, _):
+        for half in range(2):
+            relay_copy(chunk, half, 3 - my_head).wait_recv()
+        for extra in range(group):
+            out_copy(chunk * group + extra).start()
+        return 0
+
+    lax.fori_loop(0, chunks, deliver, 0)
+
+    def drain(chunk, _):
+        for stage in range(3):
+            for half in range(2):
+                pair_copy(chunk + chunks, stage, half).wait_send()
+
+        @pl.when(chunk < far_chunks)
+        def _():
+            for stage in range(3):
+                for half in range(2):
+                    pair_copy(chunk, stage, half).wait_send()
+            for extra in range(group):
+                move_copy(chunk * group + extra).wait_send()
+
+        for half in range(2):
+            gather_copy(chunk, half).wait_send()
+            relay_copy(chunk, half, near[half]).wait_send()
+        for extra in range(group):
+            step = chunk * group + extra
+
+            @pl.when(jnp.logical_and(step >= far, step != ctx_size - 2))
+            def _():
+                raw_copy(step).wait_send()
+
+            out_copy(step).wait()
+        return 0
+
+    lax.fori_loop(0, chunks, drain, 0)
+
+
+def near_exchange(sharer_k, sharer_v, recv_k, recv_v, weights, ctx_size, head_size):
+    _, block_rows, width = sharer_k.shape
+    rank = weights.shape[-1]
+    sub = block_rows // head_size
+    chunks = ctx_size // 2
+    blocks = (ctx_size, block_rows, width)
+    anywhere = pl.BlockSpec(memory_space=pl.ANY)
+    dma = pltpu.SemaphoreType.DMA
+    bf16 = jnp.bfloat16
+    return pl.pallas_call(
+        functools.partial(near_exchange_kernel, ctx_size=ctx_size, head_size=head_size),
+        in_specs=[anywhere] * 5,
+        out_specs=anywhere,
+        out_shape=jax.ShapeDtypeStruct((ctx_size, head_size, sub, rank), bf16),
+        scratch_shapes=[
+            pltpu.VMEM((2, 2 * ctx_size, block_rows, width), bf16),
+            pltpu.VMEM((4, width, 2, rank), bf16),
+            pltpu.VMEM((2, 2, width, rank), bf16),
+            pltpu.VMEM((2 * ctx_size, head_size, sub, 2 * rank), bf16),
+            pltpu.VMEM((head_size - 1, 2 * ctx_size, sub, 2 * rank), bf16),
+            pltpu.VMEM((2 * ctx_size, sub, 2 * rank), bf16),
+            pltpu.VMEM((ctx_size, sub, 2 * rank), bf16),
+            pltpu.VMEM((ctx_size, sub, 2 * rank), bf16),
+            pltpu.VMEM((ctx_size, head_size, sub, rank), bf16),
+            pltpu.VMEM((4, head_size, sub, 2 * rank), bf16),
+            dma((2, 2 * ctx_size)),
+            dma((4,)),
+            dma((2 * chunks, 6)),
+            dma((2 * chunks, 6)),
+            dma((4,)),
+            dma((4,)),
+            dma((ctx_size,)),
+            dma((ctx_size,)),
+            dma((chunks, 4)),
+            dma((chunks, 4)),
+            dma((ctx_size,)),
+        ],
+        compiler_params=pltpu.CompilerParams(
+            collective_id=1, has_side_effects=True, vmem_limit_bytes=60 * 1024 * 1024
+        ),
+        name="near_exchange",
+    )(sharer_k, sharer_v, recv_k.reshape(blocks), recv_v.reshape(blocks), weights)
+
+
 def local(
     sharer_k,
     sharer_v,
@@ -513,14 +933,10 @@
 ):
     requests, ctx_total, width = recv_k.shape
     rank = mixer_in.shape[3]
-    hidden = exchange(
-        sharer_k,
-        sharer_v,
-        recv_k,
-        recv_v,
-        mixer_in,
-        lax.axis_size("ctx"),
-        lax.axis_size("heads"),
+    ctx_size, head_size = lax.axis_size("ctx"), lax.axis_size("heads")
+    paired = head_size == 4 and ctx_size % 8 == 0
+    hidden = (near_exchange if paired else exchange)(
+        sharer_k, sharer_v, recv_k, recv_v, mixer_in, ctx_size, head_size
     )
     hidden = hidden.reshape(requests, ctx_total, rank)
     return tuple(

time: 102 us -> 80.6 us (0.79)
  Pallas kernels: 98.2 us -> 77.2 us
    pallas_call x1, Pallas kernels: 79.9 us -> 59 us  [near_exchange(): pl.pallas_call(functools.partial(near_exchange_kernel, ctx_size=ctx_size,...]
where the time goes in v1:
time: 80.6 us; the launch traced here: 80.4 us
  Pallas kernels  77.2 us (96%)
  between operations  2.01 us (2%)
  local copies, waits for them, and re-layouts  1.23 us (2%)
    pallas_call x1, Pallas kernels, near_exchange(): pl.pallas_call(functools.partial(near_exchange_kernel, ctx_size=ctx_size,...  59 us
    pallas_call x1, Pallas kernels, merge_attend(): pl.pallas_call(functools.partial(merge_attend_kernel, heads=heads, row_bl...  18.2 us

profile of v1, /device:TPU:0, one launch (start us, length us, event | category | flops | bytes accessed | tf_op | source)
XLA Modules:
  0.0 80.4 jit_solution(15006690487037403265)
XLA Ops:
  1.9 0.0 copy-start.1
  1.9 0.0 copy-start.2
  1.9 0.0 copy-start.3
  2.0 0.0 copy-start.4
  2.0 59.0 %near_exchange.1 = bf16[8,4,32,512]{3,2,1,0:T(8,128)(2,1)} custom-call(bf16[8,128,2048]{2,1,0:T(8,128)(2,1)} %sharer_k_ref.1, bf16[8,128,2048]{2,1,0:T(8,128)(2,1)} %sharer_v_ref.1, bf16[8,128,2048]{2,1,0:T(8,128)(2,1)} %bitcast.4, bf16[8,128,2048]{2,1,0:T(8,128)(2,1)} %bitcast.5, bf16[4,2048,2,512]{3,2,1,0:T(2,128)(2,1)} %w_hbm.1), custom_call_target="tpu_custom_call" | custom-call | tf_op jit(solution)/shard_map/near_exchange/pallas_call | solution.py:885
  60.9 0.0 copy-done.1
  60.9 0.0 copy-done.2
  61.0 0.0 copy-done.3
  61.0 0.0 copy-done.4
  61.0 0.0 copy-start
  61.0 1.2 %copy-done = bf16[8,4,32,512]{3,2,1,0:T(8,128)(2,1)S(1)} copy-done((bf16[8,4,32,512]{3,2,1,0:T(8,128)(2,1)S(1)}, bf16[8,4,32,512]{3,2,1,0:T(8,128)(2,1)}, u32[]{:S(2)}) %copy-start) | copy-done | bytes 1048600
  62.2 18.2 %merge_attend.1 = (bf16[1,256,2048]{2,1,0:T(8,128)(2,1)}, bf16[1,1024,2048]{2,1,0:T(8,128)(2,1)}, bf16[1,1024,2048]{2,1,0:T(8,128)(2,1)}) custom-call(s32[1]{0:T(128)S(6)} %copy.16.offset_ref, s32[1]{0:T(128)S(6)} %copy.15.length_ref, f32[2,16]{1,0:T(2,128)S(1)} %copy-done.4, bf16[1,1024,512]{2,1,0:T(8,128)(2,1)S(1)} %bitcast.3, ...), custom_call_target="tpu_custom_call" | custom-call | tf_op jit(solution)/shard_map/merge_attend/pallas_call | solution.py:106
Async XLA Ops:
  1.9 59.0 %copy-start.1 = (bf16[1,256,2048]{2,1,0:T(8,128)(2,1)S(1)}, bf16[1,256,2048]{2,1,0:T(8,128)(2,1)}, u32[]{:S(2)}) copy-start(bf16[1,256,2048]{2,1,0:T(8,128)(2,1)} %q_ref.1) | copy-start | bytes 3145732
  1.9 59.0 %copy-start.2 = (bf16[1,256,2048]{2,1,0:T(8,128)(2,1)S(1)}, bf16[1,256,2048]{2,1,0:T(8,128)(2,1)}, u32[]{:S(2)}) copy-start(bf16[1,256,2048]{2,1,0:T(8,128)(2,1)} %suf_k_ref.1) | copy-start | bytes 3145732
  1.9 59.0 %copy-start.3 = (bf16[1,256,2048]{2,1,0:T(8,128)(2,1)S(1)}, bf16[1,256,2048]{2,1,0:T(8,128)(2,1)}, u32[]{:S(2)}) copy-start(bf16[1,256,2048]{2,1,0:T(8,128)(2,1)} %suf_v_ref.1) | copy-start | bytes 3145732
  2.0 59.0 %copy-start.4 = (f32[2,16]{1,0:T(2,128)S(1)}, f32[2,16]{1,0:T(2,128)}, u32[]{:S(2)}) copy-start(f32[2,16]{1,0:T(2,128)} %gain_ref.1) | copy-start | bytes 388
  61.0 1.2 %copy-start = (bf16[8,4,32,512]{3,2,1,0:T(8,128)(2,1)S(1)}, bf16[8,4,32,512]{3,2,1,0:T(8,128)(2,1)}, u32[]{:S(2)}) copy-start(bf16[8,4,32,512]{3,2,1,0:T(8,128)(2,1)} %near_exchange.1) | copy-start | bytes 3145732
